TPU v7x, 32 devices: a whole 2x2x4 slice. The times are simulated.
32 devices in a mesh: space: 16 (over z, x, core), traj: 2 (over y).
Axes of the slice: x: 2, y: 2, z: 4, core: 2. Of those that a mesh axis runs over, the one named last changes fastest.
Arguments:
- primal_init: float32 [32, 64, 96, 128], P('traj', 'space'), may hold values from -6 to 6
- adjoint_init: float32 [32, 64, 96, 128], P('traj', 'space'), may hold values from -6 to 6
- diffusion: float32 [3, 64, 96, 128], P(None, 'space'), may hold values from 0.03 to 0.15
- velocity: float32 [3, 64, 96, 128], P(None, 'space'), may hold values from -0.12 to 0.12
- sources: int32 [2, 32], P(None, 'traj'), may hold values from 0 to 786431
Outputs:
- gram: float32 [32, 32], P(None, 'traj')
All inputs are finite; a program needn't handle non-finite values.
Results may differ from a plain program's by a relative error of at most 0.0003.
Values sent between devices are 32-bit elements; how exact they have to be, the bound alone decides.
A program may use at most 128 MiB of HBM per device.

v0:
```python
import functools
import math

import jax
import jax.numpy as jnp
from jax import lax
from jax.experimental import pallas as pl
from jax.experimental.pallas import tpu as pltpu
from jax.sharding import PartitionSpec as P

STEPS = 4
IMPULSE = 1024
GROUP = 4
LAG = 2
MESH = pl.DeviceIdType.MESH


def coefficients(dv, coef, zz):
    rows, lanes = coef.shape[2:]
    row = lax.broadcasted_iota(jnp.int32, (rows, lanes), 0)
    lane = lax.broadcasted_iota(jnp.int32, (rows, lanes), 1)

    def faces(component, plane):
        d, v = dv[0, component, plane], dv[1, component, plane]
        return d + 0.5 * v, d - 0.5 * v

    out_z, in_z = faces(0, zz + 1)
    out_z_below, in_z_below = faces(0, zz)
    out_x, in_x = faces(1, zz + 1)
    out_y, in_y = faces(2, zz + 1)
    zero = jnp.zeros((rows, lanes), jnp.float32)
    below_x = lambda value: jnp.where(row == 0, zero, pltpu.roll(value, 1, 0))
    below_y = lambda value: jnp.where(lane == 0, zero, pltpu.roll(value, 1, 1))
    centre = out_z + in_z_below + out_x + below_x(in_x) + out_y + below_y(in_y)
    coef[0, zz] = 1.0 - centre
    coef[1, zz] = in_z
    coef[2, zz] = out_z_below
    coef[3, zz] = jnp.where(row == rows - 1, zero, in_x)
    coef[4, zz] = below_x(out_x)
    coef[5, zz] = jnp.where(lane == lanes - 1, zero, in_y)
    coef[6, zz] = below_y(out_y)


def kernel(
    dims,
    src_ref,
    p_ref,
    a_ref,
    d_ref,
    v_ref,
    out_ref,
    start,
    cur,
    final,
    a_all,
    dv,
    coef,
    gred,
    part,
    part2,
    local_sem,
    chip_send,
    chip_recv,
    far_send,
    far_recv,
    relay_send,
    relay_recv,
    below_send,
    below_recv,
    a_send,
    a_recv,
    in_send,
    in_recv,
    back_send,
    back_recv,
    up_send,
    up_recv,
    down_send,
    down_recv,
    red_send,
    red_recv,
    red2_send,
    red2_recv,
):
    n, n_traj, quad = dims
    fields, planes, rows, lanes = p_ref.shape
    held = fields // quad
    deep = planes * quad
    steps = 2 * STEPS
    me = lax.axis_index("space")
    my_traj = lax.axis_index("traj")
    groups = n // quad
    mine, place = lax.div(me, quad), lax.rem(me, quad)
    beside = place + 1 - 2 * lax.rem(place, 2)
    far = lax.rem(place + 2, quad)
    has_up, has_down = mine < groups - 1, mine > 0
    above_id = {"space": jnp.minimum(me + quad, n - quad + place)}
    below_id = {"space": jnp.maximum(me - quad, place)}

    barrier = pltpu.get_barrier_semaphore()

    @pl.loop(1, n)
    def _(ahead):
        pl.semaphore_signal(
            barrier, inc=1, device_id={"space": lax.rem(me + ahead, n)}, device_id_type=MESH
        )

    for ahead in range(1, n_traj):
        pl.semaphore_signal(
            barrier,
            inc=1,
            device_id={"traj": lax.rem(my_traj + ahead, n_traj)},
            device_id_type=MESH,
        )
    pl.semaphore_wait(barrier, n - 1 + n_traj - 1)

    pair = (d_ref, v_ref)

    def faces_at(i, piece):
        return dv.at[i, :, pl.ds(1 + planes * piece, planes)]

    def send_far(i):
        return pltpu.make_async_remote_copy(
            src_ref=pair[i],
            dst_ref=faces_at(i, place),
            send_sem=far_send.at[i],
            recv_sem=far_recv.at[i],
            device_id={"space": mine * quad + far},
            device_id_type=MESH,
        )

    def send_beside(i):
        return pltpu.make_async_remote_copy(
            src_ref=pair[i],
            dst_ref=faces_at(i, place),
            send_sem=chip_send.at[i],
            recv_sem=chip_recv.at[i],
            device_id={"space": mine * quad + beside},
            device_id_type=MESH,
        )

    def relay(i):
        return pltpu.make_async_remote_copy(
            src_ref=faces_at(i, far),
            dst_ref=faces_at(i, far),
            send_sem=relay_send.at[i],
            recv_sem=relay_recv.at[i],
            device_id={"space": mine * quad + beside},
            device_id_type=MESH,
        )

    local = [
        pltpu.make_async_copy(pair[i], faces_at(i, place), local_sem.at[i]) for i in range(2)
    ]
    for i in range(2):
        send_far(i).start()
    for i in range(2):
        send_beside(i).start()
        local[i].start()

    grid = (rows, lanes)
    offset = lax.broadcasted_iota(jnp.int32, grid, 0) * lanes + lax.broadcasted_iota(
        jnp.int32, grid, 1
    )

    def with_impulse(value, source, zz):
        cell = offset + (me * planes + zz) * (rows * lanes)
        return value + jnp.where(cell == source, float(IMPULSE), 0.0)

    def hand_over(c, ahead):
        target = lax.rem(place + ahead, quad)
        return pltpu.make_async_remote_copy(
            src_ref=start.at[target * held + c],
            dst_ref=cur.at[0, c, pl.ds(1 + planes * place, planes)],
            send_sem=in_send.at[c, ahead - 1],
            recv_sem=in_recv.at[c, ahead - 1],
            device_id={"space": mine * quad + target},
            device_id_type=MESH,
        )

    def hand_back(c, ahead):
        target = lax.rem(place + ahead, quad)
        return pltpu.make_async_remote_copy(
            src_ref=cur.at[0, c, pl.ds(1 + planes * target, planes)],
            dst_ref=final.at[place * held + c],
            send_sem=back_send.at[c, ahead - 1],
            recv_sem=back_recv.at[c, ahead - 1],
            device_id={"space": mine * quad + target},
            device_id_type=MESH,
        )

    @pl.loop(0, held)
    def _(c):
        for owner in range(quad):
            f = owner * held + c
            for zz in range(planes):
                start[f, zz] = with_impulse(p_ref[f, zz], src_ref[0, f], zz)
        for ahead in (2, 1, 3):
            hand_over(c, ahead).start()
        for zz in range(planes):
            cur[0, c, 1 + planes * place + zz] = start[place * held + c, zz]

    @pl.loop(0, fields)
    def _(f):
        for zz in range(planes):
            a_all[my_traj, f, zz] = with_impulse(a_ref[f, zz], src_ref[1, f], zz)

    def gather(ahead):
        return pltpu.make_async_remote_copy(
            src_ref=a_all.at[my_traj],
            dst_ref=a_all.at[my_traj],
            send_sem=a_send.at[ahead - 1],
            recv_sem=a_recv.at[ahead - 1],
            device_id={"traj": lax.rem(my_traj + ahead, n_traj)},
            device_id_type=MESH,
        )

    for ahead in range(1, n_traj):
        gather(ahead).start()

    @pl.when(mine == 0)
    def _():
        for i in range(2):
            dv[i, 0, 0] = jnp.zeros(grid, jnp.float32)

        @pl.loop(0, held)
        def _(c):
            for slot in range(2):
                cur[slot, c, 0] = jnp.zeros(grid, jnp.float32)

    @pl.when(mine == groups - 1)
    def _():
        @pl.loop(0, held)
        def _(c):
            for slot in range(2):
                cur[slot, c, deep + 1] = jnp.zeros(grid, jnp.float32)

    for i in range(2):
        send_far(i).wait_recv()
        relay(i).start()
    for i in range(2):
        local[i].wait()
        send_beside(i).wait_recv()
        relay(i).wait_recv()

    def below(i):
        return pltpu.make_async_remote_copy(
            src_ref=dv.at[i, 0, deep],
            dst_ref=dv.at[i, 0, 0],
            send_sem=below_send.at[i],
            recv_sem=below_recv.at[i],
            device_id=above_id,
            device_id_type=MESH,
        )

    @pl.when(has_up)
    def _():
        for i in range(2):
            below(i).start()

    @pl.loop(1, deep)
    def _(zz):
        coefficients(dv, coef, zz)

    @pl.when(has_down)
    def _():
        for i in range(2):
            below(i).wait_recv()

    coefficients(dv, coef, 0)

    def halo_up(slot, c):
        return pltpu.make_async_remote_copy(
            src_ref=cur.at[slot, c, deep],
            dst_ref=cur.at[slot, c, 0],
            send_sem=up_send.at[slot, c],
            recv_sem=up_recv.at[slot, c],
            device_id=above_id,
            device_id_type=MESH,
        )

    def halo_down(slot, c):
        return pltpu.make_async_remote_copy(
            src_ref=cur.at[slot, c, 1],
            dst_ref=cur.at[slot, c, deep + 1],
            send_sem=down_send.at[slot, c],
            recv_sem=down_recv.at[slot, c],
            device_id=below_id,
            device_id_type=MESH,
        )

    def send_halos(slot, c):
        @pl.when(has_up)
        def _():
            halo_up(slot, c).start()

        @pl.when(has_down)
        def _():
            halo_down(slot, c).start()

    def wait_sent(slot, c):
        @pl.when(has_up)
        def _():
            halo_up(slot, c).wait_send()

        @pl.when(has_down)
        def _():
            halo_down(slot, c).wait_send()

    def wait_halos(slot, c):
        @pl.when(has_down)
        def _():
            halo_up(slot, c).wait_recv()

        @pl.when(has_up)
        def _():
            halo_down(slot, c).wait_recv()

    def update(slot, c, zz):
        p = cur[slot, c, zz + 1]
        cur[1 - slot, c, zz + 1] = (
            coef[0, zz] * p
            + coef[1, zz] * cur[slot, c, zz + 2]
            + coef[2, zz] * cur[slot, c, zz]
            + coef[3, zz] * pltpu.roll(p, rows - 1, 0)
            + coef[4, zz] * pltpu.roll(p, 1, 0)
            + coef[5, zz] * pltpu.roll(p, lanes - 1, 1)
            + coef[6, zz] * pltpu.roll(p, 1, 1)
        )

    @pl.loop(0, steps + 1 + (held - 1) * LAG)
    def _(turn):
        @pl.loop(0, held)
        def _(c):
            t = turn - c * LAG - 1

            @pl.when(t == -1)
            def _():
                for ahead in range(1, quad):
                    hand_over(c, ahead).wait_recv()
                send_halos(0, c)

            @pl.when((t >= 0) & (t < steps))
            def _():
                slot = lax.rem(t, 2)

                @pl.when(t > 0)
                def _():
                    wait_sent(1 - slot, c)

                wait_halos(slot, c)
                update(slot, c, 0)
                update(slot, c, deep - 1)

                @pl.when(t < steps - 1)
                def _():
                    send_halos(1 - slot, c)

                @pl.loop(1, deep - 1)
                def _(zz):
                    update(slot, c, zz)

            @pl.when(t == steps - 1)
            def _():
                for ahead in (2, 1, 3):
                    hand_back(c, ahead).start()
                for zz in range(planes):
                    final[place * held + c, zz] = cur[0, c, 1 + planes * place + zz]

    def gram_of(c, owner):
        tiles = rows // 8

        @pl.loop(0, fields // 4)
        def _(kb):
            def tile(i, sums):
                zz, first = lax.div(i, tiles), pl.multiple_of(lax.rem(i, tiles) * 8, 8)
                left = [a_all[owner, kb * 4 + k, zz, pl.ds(first, 8)] for k in range(4)]
                right = [final[j * held + c, zz, pl.ds(first, 8)] for j in range(quad)]
                return tuple(
                    sums[k * quad + j] + left[k] * right[j] for k in range(4) for j in range(quad)
                )

            zero = jnp.zeros((8, lanes), jnp.float32)
            sums = lax.fori_loop(0, planes * tiles, tile, (zero,) * (4 * quad), unroll=4)
            for k in range(4):
                for j in range(quad):
                    gred[owner * fields + kb * 4 + k, pl.ds(j * held + c, 1)] = jnp.sum(
                        sums[k * quad + j], axis=0, keepdims=True
                    )

    for ahead in range(1, n_traj):
        gather(ahead).wait_recv()

    @pl.loop(0, held)
    def _(c):
        for ahead in range(1, quad):
            hand_back(c, ahead).wait_recv()

        @pl.loop(0, n_traj)
        def _(owner):
            gram_of(c, owner)

    @pl.loop(0, held)
    def _(c):
        wait_sent(1, c)
        for ahead in range(1, quad):
            hand_over(c, ahead).wait_send()
            hand_back(c, ahead).wait_send()

    part[place] = jnp.sum(gred[...], axis=-1)

    def inside(ahead):
        return pltpu.make_async_remote_copy(
            src_ref=part.at[place],
            dst_ref=part.at[place],
            send_sem=red_send.at[ahead - 1],
            recv_sem=red_recv.at[ahead - 1],
            device_id={"space": mine * quad + lax.rem(place + ahead, quad)},
            device_id_type=MESH,
        )

    for ahead in range(1, quad):
        inside(ahead).start()
    for ahead in range(1, quad):
        inside(ahead).wait_recv()
    value = part[0]
    for i in range(1, quad):
        value = value + part[i]
    part2[mine] = value

    def across(ahead):
        return pltpu.make_async_remote_copy(
            src_ref=part2.at[mine],
            dst_ref=part2.at[mine],
            send_sem=red2_send.at[ahead - 1],
            recv_sem=red2_recv.at[ahead - 1],
            device_id={"space": lax.rem(mine + ahead, groups) * quad + place},
            device_id_type=MESH,
        )

    for ahead in range(1, groups):
        across(ahead).start()
    for ahead in range(1, groups):
        across(ahead).wait_recv()
    value = part2[0]
    for i in range(1, groups):
        value = value + part2[i]
    out_ref[...] = value / math.sqrt(n * planes * rows * lanes)

    for ahead in range(1, quad):
        inside(ahead).wait_send()
    for ahead in range(1, groups):
        across(ahead).wait_send()
    for ahead in range(1, n_traj):
        gather(ahead).wait_send()

    for i in range(2):
        send_far(i).wait_send()
        send_beside(i).wait_send()
        relay(i).wait_send()

    @pl.when(has_up)
    def _():
        for i in range(2):
            below(i).wait_send()


def solution(mesh):
    n, n_traj = mesh.shape["space"], mesh.shape["traj"]

    def on_device(primal_init, adjoint_init, diffusion, velocity, sources):
        fields, planes, rows, lanes = primal_init.shape
        quad = GROUP
        assert n % quad == 0 and fields % quad == 0
        held, deep = fields // quad, planes * quad
        total = n_traj * fields
        vmem = pl.BlockSpec(memory_space=pltpu.VMEM)
        dma = pltpu.SemaphoreType.DMA
        f32 = jnp.float32
        return pl.pallas_call(
            functools.partial(kernel, (n, n_traj, quad)),
            out_shape=jax.ShapeDtypeStruct((total, fields), f32),
            in_specs=[pl.BlockSpec(memory_space=pltpu.SMEM)] + [vmem] * 4,
            out_specs=vmem,
            scratch_shapes=[
                pltpu.VMEM((fields, planes, rows, lanes), f32),
                pltpu.VMEM((2, held, deep + 2, rows, lanes), f32),
                pltpu.VMEM((fields, planes, rows, lanes), f32),
                pltpu.VMEM((n_traj, fields, planes, rows, lanes), f32),
                pltpu.VMEM((2, 3, deep + 1, rows, lanes), f32),
                pltpu.VMEM((7, deep, rows, lanes), f32),
                pltpu.VMEM((total, fields, lanes), f32),
                pltpu.VMEM((quad, total, fields), f32),
                pltpu.VMEM((n // quad, total, fields), f32),
                *[dma((2,))] * 9,
                *[dma((max(1, n_traj - 1),))] * 2,
                *[dma((held, quad - 1))] * 4,
                *[dma((2, held))] * 4,
                *[dma((quad - 1,))] * 2,
                *[dma((max(1, n // quad - 1),))] * 2,
            ],
            compiler_params=pltpu.CompilerParams(
                collective_id=0, has_side_effects=True, vmem_limit_bytes=48 << 20
            ),
        )(sources, primal_init, adjoint_init, diffusion, velocity)

    return jax.shard_map(
        on_device,
        mesh=mesh,
        in_specs=(
            P("traj", "space", None, None),
            P("traj", "space", None, None),
            P(None, "space", None, None),
            P(None, "space", None, None),
            P(None, "traj"),
        ),
        out_specs=P(None, "traj"),
        check_vma=False,
    )
```

profile of v0, /device:TPU:0, one launch (start us, length us, event | category | flops | bytes accessed | tf_op | source)
XLA Modules:
  0.0 131.9 jit_solution(15305475734865677015)
XLA Ops:
  0.0 0.0 copy-start
  0.0 1.9 %copy-done = f32[16,4,96,128]{3,2,1,0:T(8,128)S(1)} copy-done((f32[16,4,96,128]{3,2,1,0:T(8,128)S(1)}, f32[16,4,96,128]{3,2,1,0:T(8,128)}, u32[]{:S(2)}) %copy-start) | copy-done | bytes 3145752
  1.9 0.0 copy-start.1
  1.9 1.1 copy-done.1
  3.0 0.0 copy-start.2
  3.0 1.1 copy-done.2
  4.0 0.0 copy-start.3
  4.0 0.7 copy-done.3
  4.7 126.6 %shard_map.55 = f32[32,16]{1,0:T(8,128)S(1)} custom-call(s32[2,16]{1,0:T(2,128)S(1)} %copy-done.3, f32[16,4,96,128]{3,2,1,0:T(8,128)S(1)} %copy-done, f32[16,4,96,128]{3,2,1,0:T(8,128)} %a_ref.1, f32[3,4,96,128]{3,2,1,0:T(8,128)S(1)} %copy-done.1, f32[3,4,96,128]{3,2,1,0:T(8,128)S(1)} %copy-done.2), custom_call_target="tpu_custom_call" | custom-call | tf_op jit(solution)/shard_map/pallas_call | solution.py:480
  131.3 0.7 copy.6
Async XLA Ops:
  0.0 1.9 %copy-start = (f32[16,4,96,128]{3,2,1,0:T(8,128)S(1)}, f32[16,4,96,128]{3,2,1,0:T(8,128)}, u32[]{:S(2)}) copy-start(f32[16,4,96,128]{3,2,1,0:T(8,128)} %p_ref.1) | copy-start | bytes 9437188
  1.9 1.1 copy-start.1
  3.0 1.1 copy-start.2
  4.0 0.7 copy-start.3
where the time goes:
time: 132 us
  Pallas kernels  127 us (96%)
  local copies, waits for them, and re-layouts  5.36 us (4%)
    pallas_call x1, Pallas kernels, on_device(): pl.pallas_call(functools.partial(kernel, (n, n_traj, quad)), out_shape=ja...  127 us
    unnamed x8, local copies, waits for them, and re-layouts  4.69 us

commit v1 on v0

v1 whole, which is shorter than its diff:
```python
import functools
import math

import jax
import jax.numpy as jnp
from jax import lax
from jax.experimental import pallas as pl
from jax.experimental.pallas import tpu as pltpu
from jax.sharding import PartitionSpec as P

STEPS = 4
IMPULSE = 1024
GROUP = 4
CHUNK = 2
LAG = 3
EARLY = 1
MESH = pl.DeviceIdType.MESH


def coefficients(dv, coef, zz):
    rows, lanes = coef.shape[2:]
    row = lax.broadcasted_iota(jnp.int32, (rows, lanes), 0)
    lane = lax.broadcasted_iota(jnp.int32, (rows, lanes), 1)

    def faces(component, plane):
        d, v = dv[0, component, plane], dv[1, component, plane]
        return d + 0.5 * v, d - 0.5 * v

    out_z, in_z = faces(0, zz + 1)
    out_z_below, in_z_below = faces(0, zz)
    out_x, in_x = faces(1, zz + 1)
    out_y, in_y = faces(2, zz + 1)
    zero = jnp.zeros((rows, lanes), jnp.float32)
    below_x = lambda value: jnp.where(row == 0, zero, pltpu.roll(value, 1, 0))
    below_y = lambda value: jnp.where(lane == 0, zero, pltpu.roll(value, 1, 1))
    centre = out_z + in_z_below + out_x + below_x(in_x) + out_y + below_y(in_y)
    coef[0, zz] = 1.0 - centre
    coef[1, zz] = in_z
    coef[2, zz] = out_z_below
    coef[3, zz] = jnp.where(row == rows - 1, zero, in_x)
    coef[4, zz] = below_x(out_x)
    coef[5, zz] = jnp.where(lane == lanes - 1, zero, in_y)
    coef[6, zz] = below_y(out_y)


def kernel(
    dims,
    src_ref,
    p_ref,
    a_ref,
    d_ref,
    v_ref,
    out_ref,
    cur0,
    cur1,
    final,
    a_all,
    dv,
    coef,
    gred,
    part,
    part2,
    a_local,
    same_send,
    same_recv,
    cross_send,
    cross_recv,
    relay_send,
    relay_recv,
    below_send,
    below_recv,
    a_send,
    a_recv,
    in_send,
    in_recv,
    back_send,
    back_recv,
    up_send,
    up_recv,
    down_send,
    down_recv,
    red_send,
    red_recv,
    red2_send,
    red2_recv,
    go,
):
    n, n_traj, quad, size = dims
    fields, planes, rows, lanes = p_ref.shape
    half = fields // 2
    held = half // size
    deep = planes * 2
    steps = 2 * STEPS
    cur = (cur0, cur1)
    me = lax.axis_index("space")
    my_traj = lax.axis_index("traj")
    groups = n // quad
    mine, place = lax.div(me, quad), lax.rem(me, quad)
    hx, cx = lax.div(place, 2), lax.rem(place, 2)
    sibling = {"space": mine * quad + place + 1 - 2 * cx}
    crossing = {"space": mine * quad + 2 - hx}
    parity = lax.rem(my_traj, 2)
    partner = {"traj": my_traj + 1 - 2 * parity}
    stays = hx == cx
    relays = hx != cx
    first, last = mine == 0, mine == groups - 1
    has_up = jnp.logical_not(last & (cx == 1))
    has_down = jnp.logical_not(first & (cx == 0))
    above_id = {"space": jnp.minimum(me + 1 + 2 * cx, n - 1)}
    below_id = {"space": jnp.maximum(me - 3 + 2 * cx, 0)}

    def load_adjoint(f):
        return pltpu.make_async_copy(a_ref.at[f], a_all.at[my_traj, f], a_local.at[f])

    @pl.loop(0, fields)
    def _(f):
        load_adjoint(f).start()

    barrier = pltpu.get_barrier_semaphore()

    @pl.loop(1, n)
    def _(ahead):
        pl.semaphore_signal(
            barrier, inc=1, device_id={"space": lax.rem(me + ahead, n)}, device_id_type=MESH
        )

    for ahead in range(1, n_traj):
        pl.semaphore_signal(
            barrier,
            inc=1,
            device_id={"traj": lax.rem(my_traj + ahead, n_traj)},
            device_id_type=MESH,
        )
    pl.semaphore_wait(barrier, n - 1 + n_traj - 1)

    def remote(src, dst, send, recv, target):
        return pltpu.make_async_remote_copy(
            src_ref=src,
            dst_ref=dst,
            send_sem=send,
            recv_sem=recv,
            device_id=target,
            device_id_type=MESH,
        )

    pair = (d_ref, v_ref)

    def own_planes(block):
        return pl.ds(1 + planes * block, planes)

    def keep_faces(i):
        return pltpu.make_async_copy(pair[i], dv.at[i, :, own_planes(cx)], same_recv.at[i, cx])

    def give_faces(i, block):
        return remote(
            pair[i],
            dv.at[i, :, own_planes(block)],
            same_send.at[i],
            same_recv.at[i, block],
            sibling,
        )

    def cross_faces(i, a):
        return remote(
            pair[i].at[a],
            dv.at[i, a, own_planes(cx)],
            cross_send.at[a],
            cross_recv.at[cx, a],
            crossing,
        )

    def crossed_faces(a, block):
        face = dv.at[parity, a, own_planes(block)]
        return remote(face, face, cross_send.at[a], cross_recv.at[block, a], crossing)

    def relay_faces(a, block):
        face = dv.at[parity, a, own_planes(block)]
        return remote(face, face, relay_send.at[block, a], relay_recv.at[block, a], partner)

    def relayed_faces(a, block):
        face = dv.at[1 - parity, a, own_planes(block)]
        return remote(face, face, relay_send.at[block, a], relay_recv.at[block, a], partner)

    def keep_below(i):
        return pltpu.make_async_copy(pair[i].at[0, planes - 1], dv.at[i, 0, 0], below_recv.at[i])

    def give_below(i, k, target):
        return remote(
            pair[i].at[0, planes - 1],
            dv.at[i, 0, 0],
            below_send.at[i, k],
            below_recv.at[i],
            target,
        )

    side_id = {"space": mine * quad + 3}
    over_id = [{"space": jnp.minimum(mine + 1, groups - 1) * quad + 2 * k} for k in range(2)]

    def chunk_of(which, c):
        return pl.ds(which * half + c * size, size)

    def keep_start(c):
        return pltpu.make_async_copy(
            p_ref.at[chunk_of(hx, c)],
            cur0.at[pl.ds(c * size, size), own_planes(cx)],
            in_recv.at[c, cx],
        )

    def give_start(c, block):
        return remote(
            p_ref.at[chunk_of(hx, c)],
            cur0.at[pl.ds(c * size, size), own_planes(block)],
            in_send.at[c, 0],
            in_recv.at[c, block],
            sibling,
        )

    def cross_start(c, block):
        return remote(
            p_ref.at[chunk_of(1 - hx, c)],
            cur0.at[pl.ds(c * size, size), own_planes(block)],
            in_send.at[c, 1],
            in_recv.at[c, block],
            crossing,
        )

    for a in range(3):
        for i in range(2):

            @pl.when(parity == i)
            def _():
                cross_faces(i, a).start()

    @pl.when(place == 1)
    def _():
        for i in range(2):
            keep_below(i).start()
            give_below(i, 0, side_id).start()

    @pl.when((place == 3) & jnp.logical_not(last))
    def _():
        for i in range(2):
            for k in range(2):
                give_below(i, k, over_id[k]).start()

    @pl.when(stays)
    def _():
        for i in range(2):
            keep_faces(i).start()

        @pl.loop(0, held)
        def _(c):
            keep_start(c).start()

    @pl.when(relays)
    def _():
        for i in range(2):
            give_faces(i, cx).start()

        @pl.loop(0, held)
        def _(c):
            give_start(c, cx).start()

    @pl.loop(0, held)
    def _(c):
        cross_start(c, cx).start()

    grid = (rows, lanes)
    zero_plane = jnp.zeros(grid, jnp.float32)

    def with_impulse(value, source, plane):
        offset = lax.broadcasted_iota(jnp.int32, grid, 0) * lanes + lax.broadcasted_iota(
            jnp.int32, grid, 1
        )
        return value + jnp.where(offset == source - plane * (rows * lanes), float(IMPULSE), 0.0)

    def gather(ahead, f):
        return remote(
            a_all.at[my_traj, f],
            a_all.at[my_traj, f],
            a_send.at[ahead - 1, f],
            a_recv.at[ahead - 1, f],
            {"traj": lax.rem(my_traj + ahead, n_traj)},
        )

    def gathered(ahead, f):
        owner = lax.rem(my_traj + n_traj - ahead, n_traj)
        return remote(
            a_all.at[owner, f],
            a_all.at[owner, f],
            a_send.at[ahead - 1, f],
            a_recv.at[ahead - 1, f],
            {"traj": lax.rem(my_traj + ahead, n_traj)},
        )

    @pl.loop(0, fields)
    def _(f):
        load_adjoint(f).wait()
        for zz in range(planes):
            a_all[my_traj, f, zz] = with_impulse(
                a_all[my_traj, f, zz], src_ref[1, f], me * planes + zz
            )

        @pl.when((f >= 1) & (f <= EARLY))
        def _():
            for ahead in range(1, n_traj):
                gather(ahead, f - 1).start()

    @pl.when(first & (cx == 0))
    def _():
        for i in range(2):
            dv[i, 0, 0] = zero_plane

        @pl.loop(0, half)
        def _(f):
            for slot in range(2):
                cur[slot][f, 0] = zero_plane

    @pl.when(last & (cx == 1))
    def _():
        @pl.loop(0, half)
        def _(f):
            for slot in range(2):
                cur[slot][f, deep + 1] = zero_plane

    @pl.when(relays)
    def _():
        for a in range(3):
            for block in range(2):
                crossed_faces(a, block).wait_recv()
                relay_faces(a, block).start()
        pl.semaphore_signal(go, inc=1, device_id=sibling, device_id_type=MESH)

    @pl.when(stays)
    def _():
        for i in range(2):
            keep_faces(i).wait()
            give_faces(i, 1 - cx).wait_recv()
        pl.semaphore_wait(go, 1)

    @pl.loop(EARLY, fields)
    def _(f):
        for ahead in range(1, n_traj):
            gather(ahead, f).start()

    @pl.when(place == 1)
    def _():
        for i in range(2):
            keep_below(i).wait()

    @pl.when((place == 3) | ((cx == 0) & jnp.logical_not(first)))
    def _():
        for i in range(2):
            give_below(i, 0, side_id).wait_recv()

    @pl.when(relays)
    def _():
        for a in range(3):
            for block in range(2):
                relayed_faces(a, block).wait_recv()

    @pl.loop(0, deep)
    def _(zz):
        coefficients(dv, coef, zz)

    def halo_up(slot, c):
        return remote(
            cur[slot].at[pl.ds(c * size, size), deep],
            cur[slot].at[pl.ds(c * size, size), 0],
            up_send.at[slot, c],
            up_recv.at[slot, c],
            above_id,
        )

    def halo_down(slot, c):
        return remote(
            cur[slot].at[pl.ds(c * size, size), 1],
            cur[slot].at[pl.ds(c * size, size), deep + 1],
            down_send.at[slot, c],
            down_recv.at[slot, c],
            below_id,
        )

    def send_halos(slot, c):
        @pl.when(has_up)
        def _():
            halo_up(slot, c).start()

        @pl.when(has_down)
        def _():
            halo_down(slot, c).start()

    def wait_sent(slot, c):
        @pl.when(has_up)
        def _():
            halo_up(slot, c).wait_send()

        @pl.when(has_down)
        def _():
            halo_down(slot, c).wait_send()

    def wait_halos(slot, c):
        @pl.when(has_down)
        def _():
            halo_up(slot, c).wait_recv()

        @pl.when(has_up)
        def _():
            halo_down(slot, c).wait_recv()

    tiles = rows // 8

    def update(slot, c, zz):
        old, new = cur[slot], cur[1 - slot]
        for r in range(tiles):
            at = pl.ds(8 * r, 8)
            k = [coef[i, zz, at] for i in range(7)]
            for i in range(size):
                f = c * size + i
                p = old[f, zz + 1, at]
                if r > 0:
                    before = old[f, zz + 1, pl.ds(8 * r - 1, 8)]
                else:
                    before = pltpu.roll(p, 1, 0)
                if r < tiles - 1:
                    after = old[f, zz + 1, pl.ds(8 * r + 1, 8)]
                else:
                    after = pltpu.roll(p, 7, 0)
                new[f, zz + 1, at] = (
                    k[5] * pltpu.roll(p, lanes - 1, 1)
                    + k[6] * pltpu.roll(p, 1, 1)
                    + k[0] * p
                    + k[1] * old[f, zz + 2, at]
                    + k[2] * old[f, zz, at]
                    + k[3] * after
                    + k[4] * before
                )

    def add_impulses(c, zz):
        for i in range(size):
            f = c * size + i
            cur0[f, zz + 1] = with_impulse(
                cur0[f, zz + 1],
                src_ref[0, hx * half + f],
                (mine * 2 + cx) * deep + zz,
            )

    def wait_start(c):
        @pl.when(stays)
        def _():
            keep_start(c).wait()
            give_start(c, 1 - cx).wait_recv()

        @pl.when(relays)
        def _():
            for block in range(2):
                cross_start(c, block).wait_recv()

    def keep_final(c):
        return pltpu.make_async_copy(
            cur0.at[pl.ds(c * size, size), own_planes(cx)],
            final.at[chunk_of(hx, c)],
            back_recv.at[c, hx],
        )

    def give_final(c, b, which):
        return remote(
            cur0.at[pl.ds(c * size, size), own_planes(b)],
            final.at[chunk_of(which, c)],
            back_send.at[c, b],
            back_recv.at[c, which],
            {"space": mine * quad + cx * 2 + b},
        )

    @pl.loop(0, steps + 1 + (held - 1) * LAG)
    def _(turn):
        @pl.loop(0, held)
        def _(c):
            t = turn - c * LAG - 1

            @pl.when(t == -1)
            def _():
                wait_start(c)
                add_impulses(c, 0)
                add_impulses(c, deep - 1)
                send_halos(0, c)

                @pl.loop(1, deep - 1)
                def _(zz):
                    add_impulses(c, zz)

            for slot in range(2):

                @pl.when((t >= 0) & (t < steps) & (lax.rem(t, 2) == slot))
                def _():
                    @pl.when(t > 0)
                    def _():
                        wait_sent(1 - slot, c)

                    wait_halos(slot, c)

                    @pl.loop(0, 2)
                    def _(side):
                        update(slot, c, side * (deep - 1))

                    @pl.when(t < steps - 1)
                    def _():
                        send_halos(1 - slot, c)

                    @pl.loop(1, deep - 1)
                    def _(zz):
                        update(slot, c, zz)

            @pl.when(t == steps - 1)
            def _():
                @pl.when(stays)
                def _():
                    give_final(c, 1 - cx, hx).start()
                    keep_final(c).start()

                @pl.when(relays)
                def _():
                    for b in range(2):
                        give_final(c, b, hx).start()

    def wait_final(c):
        @pl.when(stays)
        def _():
            keep_final(c).wait()
            give_final(c, 1 - cx, 1 - hx).wait_recv()

        @pl.when(relays)
        def _():
            for which in range(2):
                give_final(c, 0, which).wait_recv()

    def gram_of(c, owner, kb):
        columns = [which * half + c * size + i for which in range(2) for i in range(size)]

        def plane(zz, sums):
            def tile(i, sums):
                at = pl.ds(pl.multiple_of(i * 8, 8), 8)
                left = [a_all[owner, kb * 4 + k, zz, at] for k in range(4)]
                right = [final[j, zz, at] for j in columns]
                return tuple(
                    sums[k * len(columns) + j] + left[k] * right[j]
                    for k in range(4)
                    for j in range(len(columns))
                )

            return lax.fori_loop(0, tiles, tile, sums, unroll=tiles)

        zero = jnp.zeros((8, lanes), jnp.float32)
        sums = lax.fori_loop(0, planes, plane, (zero,) * (4 * len(columns)))
        for k in range(4):
            for j, column in enumerate(columns):
                gred[owner * fields + kb * 4 + k, pl.ds(column, 1)] = jnp.sum(
                    sums[k * len(columns) + j], axis=0, keepdims=True
                )

    @pl.loop(0, held)
    def _(c):
        wait_final(c)

        @pl.loop(0, fields // 4)
        def _(kb):
            gram_of(c, my_traj, kb)

        for ahead in range(1, n_traj):

            @pl.loop(0, fields // 4)
            def _(kb):
                @pl.when(c == 0)
                def _():
                    for k in range(4):
                        gathered(ahead, kb * 4 + k).wait_recv()

                gram_of(c, lax.rem(my_traj + n_traj - ahead, n_traj), kb)

    part[place] = jnp.sum(gred[...], axis=-1)

    def inside(ahead):
        return pltpu.make_async_remote_copy(
            src_ref=part.at[place],
            dst_ref=part.at[place],
            send_sem=red_send.at[ahead - 1],
            recv_sem=red_recv.at[ahead - 1],
            device_id={"space": mine * quad + lax.rem(place + ahead, quad)},
            device_id_type=MESH,
        )

    for ahead in range(1, quad):
        inside(ahead).start()
    for ahead in range(1, quad):
        inside(ahead).wait_recv()
    value = part[0]
    for i in range(1, quad):
        value = value + part[i]
    part2[mine] = value

    def across(ahead):
        return pltpu.make_async_remote_copy(
            src_ref=part2.at[mine],
            dst_ref=part2.at[mine],
            send_sem=red2_send.at[ahead - 1],
            recv_sem=red2_recv.at[ahead - 1],
            device_id={"space": lax.rem(mine + ahead, groups) * quad + place},
            device_id_type=MESH,
        )

    for ahead in range(1, groups):
        across(ahead).start()
    for ahead in range(1, groups):
        across(ahead).wait_recv()
    value = part2[0]
    for i in range(1, groups):
        value = value + part2[i]
    out_ref[...] = value / math.sqrt(n * planes * rows * lanes)

    for ahead in range(1, quad):
        inside(ahead).wait_send()
    for ahead in range(1, groups):
        across(ahead).wait_send()

    @pl.loop(0, fields)
    def _(f):
        for ahead in range(1, n_traj):
            gather(ahead, f).wait_send()

    for a in range(3):
        crossed_faces(a, cx).wait_send()

    @pl.when(place == 1)
    def _():
        for i in range(2):
            give_below(i, 0, side_id).wait_send()

    @pl.when((place == 3) & jnp.logical_not(last))
    def _():
        for i in range(2):
            for k in range(2):
                give_below(i, k, over_id[k]).wait_send()

    @pl.when(relays)
    def _():
        for i in range(2):
            give_faces(i, cx).wait_send()
        for a in range(3):
            for block in range(2):
                relay_faces(a, block).wait_send()

    @pl.loop(0, held)
    def _(c):
        wait_sent(1, c)
        cross_start(c, cx).wait_send()

        @pl.when(stays)
        def _():
            give_final(c, 1 - cx, hx).wait_send()

        @pl.when(relays)
        def _():
            give_start(c, cx).wait_send()
            for b in range(2):
                give_final(c, b, hx).wait_send()


def solution(mesh):
    n, n_traj = mesh.shape["space"], mesh.shape["traj"]

    def on_device(primal_init, adjoint_init, diffusion, velocity, sources):
        fields, planes, rows, lanes = primal_init.shape
        quad = GROUP
        assert n % quad == 0 and n_traj % 2 == 0 and fields % (2 * CHUNK) == 0
        size = CHUNK
        half, deep = fields // 2, planes * 2
        held = half // size
        total = n_traj * fields
        hbm = pl.BlockSpec(memory_space=pltpu.HBM)
        dma = pltpu.SemaphoreType.DMA
        f32 = jnp.float32
        others = max(1, n_traj - 1)
        return pl.pallas_call(
            functools.partial(kernel, (n, n_traj, quad, size)),
            out_shape=jax.ShapeDtypeStruct((total, fields), f32),
            in_specs=[pl.BlockSpec(memory_space=pltpu.SMEM)] + [hbm] * 4,
            out_specs=pl.BlockSpec(memory_space=pltpu.VMEM),
            scratch_shapes=[
                *[pltpu.VMEM((half, deep + 2, rows, lanes), f32)] * 2,
                pltpu.VMEM((fields, planes, rows, lanes), f32),
                pltpu.VMEM((n_traj, fields, planes, rows, lanes), f32),
                pltpu.VMEM((2, 3, deep + 1, rows, lanes), f32),
                pltpu.VMEM((7, deep, rows, lanes), f32),
                pltpu.VMEM((total, fields, lanes), f32),
                pltpu.VMEM((quad, total, fields), f32),
                pltpu.VMEM((n // quad, total, fields), f32),
                dma((fields,)),
                dma((2,)),
                dma((2, 2)),
                dma((3,)),
                *[dma((2, 3))] * 3,
                dma((2, 2)),
                dma((2,)),
                *[dma((others, fields))] * 2,
                *[dma((held, 2))] * 4,
                *[dma((2, held))] * 4,
                *[dma((quad - 1,))] * 2,
                *[dma((max(1, n // quad - 1),))] * 2,
                pltpu.SemaphoreType.REGULAR,
            ],
            compiler_params=pltpu.CompilerParams(
                collective_id=0, has_side_effects=True, vmem_limit_bytes=67043328
            ),
        )(sources, primal_init, adjoint_init, diffusion, velocity)

    return jax.shard_map(
        on_device,
        mesh=mesh,
        in_specs=(
            P("traj", "space", None, None),
            P("traj", "space", None, None),
            P(None, "space", None, None),
            P(None, "space", None, None),
            P(None, "traj"),
        ),
        out_specs=P(None, "traj"),
        check_vma=False,
    )
```

time: 132 us -> 120 us (0.909)
  Pallas kernels: 127 us -> 118 us
  local copies, waits for them, and re-layouts: 5.36 us -> 1.39 us
    pallas_call x1, Pallas kernels: 127 us -> 118 us  [on_device(): pl.pallas_call(functools.partial(kernel, (n, n_traj, quad, size)), out_sh...]
    unnamed x8 -> x0, local copies, waits for them, and re-layouts: 4.69 us -> none
where the time goes in v1:
time: 120 us; the launch traced here: 119 us
  Pallas kernels  118 us (98%)
  local copies, waits for them, and re-layouts  1.39 us (1%)
    pallas_call x1, Pallas kernels, on_device(): pl.pallas_call(functools.partial(kernel, (n, n_traj, quad, size)), out_sh...  118 us

profile of v1, /device:TPU:0, one launch (start us, length us, event | category | flops | bytes accessed | tf_op | source)
XLA Modules:
  0.0 119.4 jit_solution(4828075719038578873)
XLA Ops:
  0.0 118.0 %shard_map.55 = f32[32,16]{1,0:T(8,128)} custom-call(s32[2,16]{1,0:T(2,128)} %src_ref.1, f32[16,4,96,128]{3,2,1,0:T(8,128)} %p_ref.1, f32[16,4,96,128]{3,2,1,0:T(8,128)} %a_ref.1, f32[3,4,96,128]{3,2,1,0:T(8,128)} %d_ref.1, f32[3,4,96,128]{3,2,1,0:T(8,128)} %v_ref.1), custom_call_target="tpu_custom_call" | custom-call | tf_op jit(solution)/shard_map/pallas_call | solution.py:683
  118.0 1.4 %copy.6 = f32[32,16]{0,1:T(8,128)} copy(f32[32,16]{1,0:T(8,128)} %shard_map.55) | data formatting | bytes 4096 | tf_op jit(solution)/shard_map/pallas_call | solution.py:683

commit v2 on v1

--- a/solution.py
+++ b/solution.py
@@ -11,8 +11,8 @@
 STEPS = 4
 IMPULSE = 1024
 GROUP = 4
-CHUNK = 2
-LAG = 3
+CHUNK = 1
+LAG = 1
 EARLY = 1
 MESH = pl.DeviceIdType.MESH
 
@@ -410,31 +410,31 @@
 
     tiles = rows // 8
 
-    def update(slot, c, zz):
+    def update(slot, c, zs):
         old, new = cur[slot], cur[1 - slot]
         for r in range(tiles):
             at = pl.ds(8 * r, 8)
-            k = [coef[i, zz, at] for i in range(7)]
-            for i in range(size):
-                f = c * size + i
-                p = old[f, zz + 1, at]
-                if r > 0:
-                    before = old[f, zz + 1, pl.ds(8 * r - 1, 8)]
-                else:
-                    before = pltpu.roll(p, 1, 0)
-                if r < tiles - 1:
-                    after = old[f, zz + 1, pl.ds(8 * r + 1, 8)]
-                else:
-                    after = pltpu.roll(p, 7, 0)
-                new[f, zz + 1, at] = (
-                    k[5] * pltpu.roll(p, lanes - 1, 1)
-                    + k[6] * pltpu.roll(p, 1, 1)
-                    + k[0] * p
-                    + k[1] * old[f, zz + 2, at]
-                    + k[2] * old[f, zz, at]
-                    + k[3] * after
-                    + k[4] * before
-                )
+            for f in [c * size + i for i in range(size)]:
+                for zz in zs:
+                    k = [coef[i, zz, at] for i in range(7)]
+                    p = old[f, zz + 1, at]
+                    if r > 0:
+                        before = old[f, zz + 1, pl.ds(8 * r - 1, 8)]
+                    else:
+                        before = pltpu.roll(p, 1, 0)
+                    if r < tiles - 1:
+                        after = old[f, zz + 1, pl.ds(8 * r + 1, 8)]
+                    else:
+                        after = pltpu.roll(p, 7, 0)
+                    new[f, zz + 1, at] = (
+                        k[5] * pltpu.roll(p, lanes - 1, 1)
+                        + k[6] * pltpu.roll(p, 1, 1)
+                        + k[0] * p
+                        + k[1] * old[f, zz + 2, at]
+                        + k[2] * old[f, zz, at]
+                        + k[3] * after
+                        + k[4] * before
+                    )
 
     def add_impulses(c, zz):
         for i in range(size):
@@ -499,17 +499,15 @@
 
                     wait_halos(slot, c)
 
-                    @pl.loop(0, 2)
-                    def _(side):
-                        update(slot, c, side * (deep - 1))
+                    update(slot, c, (0, deep - 1))
 
                     @pl.when(t < steps - 1)
                     def _():
                         send_halos(1 - slot, c)
 
-                    @pl.loop(1, deep - 1)
+                    @pl.loop(1, deep - 1, step=2)
                     def _(zz):
-                        update(slot, c, zz)
+                        update(slot, c, (zz, zz + 1))
 
             @pl.when(t == steps - 1)
             def _():
@@ -558,24 +556,49 @@
                     sums[k * len(columns) + j], axis=0, keepdims=True
                 )
 
-    @pl.loop(0, held)
+    blocks = fields // 4
+
+    def gram_own(c):
+        @pl.loop(0, blocks)
+        def _(kb):
+            gram_of(c, my_traj, kb)
+
+    def gram_other(ahead, c, kb):
+        gram_of(c, lax.rem(my_traj + n_traj - ahead, n_traj), kb)
+
+    def wait_block(ahead, kb):
+        for k in range(4):
+            gathered(ahead, kb * 4 + k).wait_recv()
+
+    @pl.loop(0, held - 1)
     def _(c):
         wait_final(c)
-
-        @pl.loop(0, fields // 4)
-        def _(kb):
-            gram_of(c, my_traj, kb)
-
+        gram_own(c)
         for ahead in range(1, n_traj):
 
-            @pl.loop(0, fields // 4)
+            @pl.loop(0, blocks - 1)
             def _(kb):
                 @pl.when(c == 0)
                 def _():
-                    for k in range(4):
-                        gathered(ahead, kb * 4 + k).wait_recv()
-
-                gram_of(c, lax.rem(my_traj + n_traj - ahead, n_traj), kb)
+                    wait_block(ahead, kb)
+
+                gram_other(ahead, c, kb)
+
+    for ahead in range(1, n_traj):
+        wait_block(ahead, blocks - 1)
+
+    @pl.loop(0, held - 1)
+    def _(c):
+        for ahead in range(1, n_traj):
+            gram_other(ahead, c, blocks - 1)
+
+    wait_final(held - 1)
+    gram_own(held - 1)
+    for ahead in range(1, n_traj):
+
+        @pl.loop(0, blocks)
+        def _(kb):
+            gram_other(ahead, held - 1, kb)
 
     part[place] = jnp.sum(gred[...], axis=-1)
 
@@ -671,7 +694,7 @@
     def on_device(primal_init, adjoint_init, diffusion, velocity, sources):
         fields, planes, rows, lanes = primal_init.shape
         quad = GROUP
-        assert n % quad == 0 and n_traj % 2 == 0 and fields % (2 * CHUNK) == 0
+        assert n % quad == 0 and n_traj % 2 == 0 and fields % (4 * CHUNK) == 0
         size = CHUNK
         half, deep = fields // 2, planes * 2
         held = half // size

time: 120 us -> 106 us (0.88)
  Pallas kernels: 118 us -> 104 us
    pallas_call x1, Pallas kernels: 118 us -> 104 us  [on_device(): pl.pallas_call(functools.partial(kernel, (n, n_traj, quad, size)), out_sh...]
where the time goes in v2:
time: 106 us
  Pallas kernels  104 us (98%)
  local copies, waits for them, and re-layouts  1.39 us (1%)
    pallas_call x1, Pallas kernels, on_device(): pl.pallas_call(functools.partial(kernel, (n, n_traj, quad, size)), out_sh...  104 us

profile of v2, /device:TPU:0, one launch (start us, length us, event | category | flops | bytes accessed | tf_op | source)
XLA Modules:
  0.0 105.8 jit_solution(4062232965867601632)
XLA Ops:
  0.0 104.4 %shard_map.55 = f32[32,16]{1,0:T(8,128)} custom-call(s32[2,16]{1,0:T(2,128)} %src_ref.1, f32[16,4,96,128]{3,2,1,0:T(8,128)} %p_ref.1, f32[16,4,96,128]{3,2,1,0:T(8,128)} %a_ref.1, f32[3,4,96,128]{3,2,1,0:T(8,128)} %d_ref.1, f32[3,4,96,128]{3,2,1,0:T(8,128)} %v_ref.1), custom_call_target="tpu_custom_call" | custom-call | tf_op jit(solution)/shard_map/pallas_call | solution.py:706
  104.4 1.4 %copy.6 = f32[32,16]{0,1:T(8,128)} copy(f32[32,16]{1,0:T(8,128)} %shard_map.55) | data formatting | bytes 4096 | tf_op jit(solution)/shard_map/pallas_call | solution.py:706

commit v3 on v2

--- a/solution.py
+++ b/solution.py
@@ -58,8 +58,8 @@
     dv,
     coef,
     gred,
+    box,
     part,
-    part2,
     a_local,
     same_send,
     same_recv,
@@ -81,8 +81,6 @@
     down_recv,
     red_send,
     red_recv,
-    red2_send,
-    red2_recv,
     go,
 ):
     n, n_traj, quad, size = dims
@@ -338,10 +336,13 @@
             give_faces(i, 1 - cx).wait_recv()
         pl.semaphore_wait(go, 1)
 
-    @pl.loop(EARLY, fields)
-    def _(f):
-        for ahead in range(1, n_traj):
-            gather(ahead, f).start()
+    def send_adjoint():
+        @pl.loop(EARLY, fields)
+        def _(f):
+            for ahead in range(1, n_traj):
+                gather(ahead, f).start()
+
+    pl.when(relays)(send_adjoint)
 
     @pl.when(place == 1)
     def _():
@@ -477,6 +478,7 @@
         @pl.loop(0, held)
         def _(c):
             t = turn - c * LAG - 1
+            pl.when((turn == 1) & (c == 0) & stays)(send_adjoint)
 
             @pl.when(t == -1)
             def _():
@@ -600,50 +602,41 @@
         def _(kb):
             gram_other(ahead, held - 1, kb)
 
-    part[place] = jnp.sum(gred[...], axis=-1)
-
-    def inside(ahead):
-        return pltpu.make_async_remote_copy(
-            src_ref=part.at[place],
-            dst_ref=part.at[place],
-            send_sem=red_send.at[ahead - 1],
-            recv_sem=red_recv.at[ahead - 1],
-            device_id={"space": mine * quad + lax.rem(place + ahead, quad)},
-            device_id_type=MESH,
-        )
-
-    for ahead in range(1, quad):
-        inside(ahead).start()
-    for ahead in range(1, quad):
-        inside(ahead).wait_recv()
-    value = part[0]
-    for i in range(1, quad):
-        value = value + part[i]
-    part2[mine] = value
-
-    def across(ahead):
-        return pltpu.make_async_remote_copy(
-            src_ref=part2.at[mine],
-            dst_ref=part2.at[mine],
-            send_sem=red2_send.at[ahead - 1],
-            recv_sem=red2_recv.at[ahead - 1],
-            device_id={"space": lax.rem(mine + ahead, groups) * quad + place},
-            device_id_type=MESH,
-        )
-
-    for ahead in range(1, groups):
-        across(ahead).start()
-    for ahead in range(1, groups):
-        across(ahead).wait_recv()
-    value = part2[0]
-    for i in range(1, groups):
-        value = value + part2[i]
-    out_ref[...] = value / math.sqrt(n * planes * rows * lanes)
-
-    for ahead in range(1, quad):
-        inside(ahead).wait_send()
-    for ahead in range(1, groups):
-        across(ahead).wait_send()
+    stacks = out_ref.shape[0] // 8
+    pitch = lanes // stacks
+    box[...] = jnp.zeros(box.shape, jnp.float32)
+    box[:, pl.ds(0, fields)] = jnp.sum(gred[...], axis=-1)
+    packed = box[pl.ds(0, 8)]
+    for i in range(1, stacks):
+        packed = packed + pltpu.roll(box[pl.ds(8 * i, 8)], pitch * i, 1)
+    part[me] = packed
+
+    def share(ahead):
+        return remote(
+            part.at[me],
+            part.at[me],
+            red_send.at[ahead - 1],
+            red_recv.at[ahead - 1],
+            {"space": lax.rem(me + ahead, n)},
+        )
+
+    @pl.loop(1, n)
+    def _(ahead):
+        share(ahead).start()
+
+    @pl.loop(1, n)
+    def _(ahead):
+        share(ahead).wait_recv()
+
+    value = lax.fori_loop(1, n, lambda i, total: total + part[i], part[0])
+    value = value / math.sqrt(n * planes * rows * lanes)
+    for i in range(stacks):
+        shifted = pltpu.roll(value, (lanes - pitch * i) % lanes, 1) if i else value
+        out_ref[pl.ds(8 * i, 8)] = shifted[:, :fields]
+
+    @pl.loop(1, n)
+    def _(ahead):
+        share(ahead).wait_send()
 
     @pl.loop(0, fields)
     def _(f):
@@ -694,11 +687,12 @@
     def on_device(primal_init, adjoint_init, diffusion, velocity, sources):
         fields, planes, rows, lanes = primal_init.shape
         quad = GROUP
+        total = n_traj * fields
+        assert total % 8 == 0 and fields * total <= 8 * lanes
         assert n % quad == 0 and n_traj % 2 == 0 and fields % (4 * CHUNK) == 0
         size = CHUNK
         half, deep = fields // 2, planes * 2
         held = half // size
-        total = n_traj * fields
         hbm = pl.BlockSpec(memory_space=pltpu.HBM)
         dma = pltpu.SemaphoreType.DMA
         f32 = jnp.float32
@@ -715,8 +709,8 @@
                 pltpu.VMEM((2, 3, deep + 1, rows, lanes), f32),
                 pltpu.VMEM((7, deep, rows, lanes), f32),
                 pltpu.VMEM((total, fields, lanes), f32),
-                pltpu.VMEM((quad, total, fields), f32),
-                pltpu.VMEM((n // quad, total, fields), f32),
+                pltpu.VMEM((total, lanes), f32),
+                pltpu.VMEM((n, 8, lanes), f32),
                 dma((fields,)),
                 dma((2,)),
                 dma((2, 2)),
@@ -727,8 +721,7 @@
                 *[dma((others, fields))] * 2,
                 *[dma((held, 2))] * 4,
                 *[dma((2, held))] * 4,
-                *[dma((quad - 1,))] * 2,
-                *[dma((max(1, n // quad - 1),))] * 2,
+                *[dma((n - 1,))] * 2,
                 pltpu.SemaphoreType.REGULAR,
             ],
             compiler_params=pltpu.CompilerParams(

time: 106 us -> 103 us (0.972)
  Pallas kernels: 104 us -> 101 us
    pallas_call x1, Pallas kernels: 104 us -> 101 us  [on_device(): pl.pallas_call(functools.partial(kernel, (n, n_traj, quad, size)), out_sh...]
where the time goes in v3:
time: 103 us
  Pallas kernels  101 us (98%)
  local copies, waits for them, and re-layouts  1.39 us (1%)
    pallas_call x1, Pallas kernels, on_device(): pl.pallas_call(functools.partial(kernel, (n, n_traj, quad, size)), out_sh...  101 us

profile of v3, /device:TPU:0, one launch (start us, length us, event | category | flops | bytes accessed | tf_op | source)
XLA Modules:
  0.0 102.6 jit_solution(3071301100031593893)
XLA Ops:
  0.0 101.2 %shard_map.55 = f32[32,16]{1,0:T(8,128)} custom-call(s32[2,16]{1,0:T(2,128)} %src_ref.1, f32[16,4,96,128]{3,2,1,0:T(8,128)} %p_ref.1, f32[16,4,96,128]{3,2,1,0:T(8,128)} %a_ref.1, f32[3,4,96,128]{3,2,1,0:T(8,128)} %d_ref.1, f32[3,4,96,128]{3,2,1,0:T(8,128)} %v_ref.1), custom_call_target="tpu_custom_call" | custom-call | tf_op jit(solution)/shard_map/pallas_call | solution.py:700
  101.2 1.4 %copy.6 = f32[32,16]{0,1:T(8,128)} copy(f32[32,16]{1,0:T(8,128)} %shard_map.55) | data formatting | bytes 4096 | tf_op jit(solution)/shard_map/pallas_call | solution.py:700
